TPU v7x, 32 devices: a whole 2x2x4 slice. The times are simulated.
32 devices in a mesh: seq: 8 (over z, y), kvh: 4 (over x, core).
Axes of the slice: x: 2, y: 2, z: 4, core: 2. Of those that a mesh axis runs over, the one named last changes fastest.
Arguments:
- queries: bfloat16 [1024, 8192], P('seq', 'kvh'), may hold values from -100 to 100
- keys: bfloat16 [1024, 1024], P('seq', 'kvh'), may hold values from -4 to 4
- values: bfloat16 [1024, 1024], P('seq', 'kvh'), may hold values from -6 to 6
- segments: int32 [1024], P('seq'), may hold values from 0 to 2, never falling along the last dimension, each value on 1 to 640 neighbouring positions
- basis: bfloat16 [8, 2, 128, 32], P('kvh'), may hold values from -0.5 to 0.5
Outputs:
- attention: bfloat16 [1024, 8192], P('seq', 'kvh')
- latents: bfloat16 [1024, 512], P('seq', 'kvh')
- captured: float32 [8, 2, 32, 32], P('kvh')
- share: float32 [8, 2], P('kvh')
Inputs may be any that keep to these rules, and one draw needn't show every extreme that they name: `segments`: document ids never fall along the sequence, and each document has at most 640 tokens.
All inputs are finite; a program needn't handle non-finite values.
Results may differ from a plain program's by a relative error of at most 0.004.
Values may be sent and summed in bfloat16 or wider, within the bound.
A program may use at most 64 MiB of HBM per device.

v0:
```python
import jax
import jax.numpy as jnp
from jax import lax
from jax.sharding import PartitionSpec as P

HD = 128
QH = 64
KVH = 8
RANK = 32


def shifted(block, axis, distance):
    devices = range(lax.axis_size(axis))
    route = [(i - distance, i) for i in devices if i - distance in devices]
    return lax.ppermute(block, axis, route)


def project(basis_f32, gram):
    return jnp.einsum(
        "hcdr,hcde,hces->hcrs", basis_f32, gram, basis_f32, precision=lax.Precision.HIGHEST
    )


def body(queries, keys, values, segments, basis):
    tok_rows = queries.shape[0]
    local_heads = keys.shape[1] // HD
    per_group = QH // KVH
    cycle_index = lax.axis_index("seq")
    cycle_size = lax.axis_size("seq")
    query_heads = queries.reshape(tok_rows, local_heads, per_group, HD)
    query_pos = cycle_index * tok_rows + jnp.arange(tok_rows, dtype=jnp.int32)
    seg_here = segments.astype(jnp.float32)
    score_scale = float(HD) ** (-0.5)

    def attend(carried, kv_block, key_start, usable):
        key_block, value_block, seg_block = kv_block
        key_count = key_block.shape[0]
        key_width = min(key_count, 512)
        part_count = key_count // key_width
        key_parts = key_block.reshape(part_count, key_width, local_heads, HD)
        value_parts = value_block.reshape(part_count, key_width, local_heads, HD)
        seg_parts = seg_block.reshape(part_count, key_width)
        usable = jnp.asarray(usable)

        def one_part(carried, inputs):
            key_part, value_part, seg_part, number = inputs
            first_key = key_start + number * key_width
            key_pos = first_key + jnp.arange(key_width, dtype=jnp.int32)
            seg_keys = seg_part.astype(jnp.float32)
            running_max, running_sum, weighted = carried
            allowed = (
                (key_pos[None, :] <= query_pos[:, None])
                & (seg_keys[None, :] == seg_here[:, None])
                & usable
            )
            scores = (
                jnp.einsum(
                    "tgjd,sgd->gjts", query_heads, key_part, preferred_element_type=jnp.float32
                )
                * score_scale
            )
            scores = jnp.where(allowed[None, None], scores, -1e30)
            new_max = jnp.maximum(running_max, jnp.max(scores, axis=-1))
            weights = jnp.where(allowed[None, None], jnp.exp(scores - new_max[..., None]), 0.0)
            factor = jnp.exp(running_max - new_max)
            running_sum = running_sum * factor + jnp.sum(weights, axis=-1)
            weighted = weighted * factor[..., None] + jnp.einsum(
                "gjts,sgd->gjtd",
                weights.astype(jnp.bfloat16),
                value_part,
                preferred_element_type=jnp.float32,
            )
            carried = (new_max, running_sum, weighted)
            return (carried, None)

        carried, unused = lax.scan(
            one_part,
            carried,
            (key_parts, value_parts, seg_parts, jnp.arange(part_count, dtype=jnp.int32)),
        )
        return carried

    initial = (
        jnp.full((local_heads, per_group, tok_rows), -1e30, jnp.float32),
        jnp.zeros((local_heads, per_group, tok_rows), jnp.float32),
        jnp.zeros((local_heads, per_group, tok_rows, HD), jnp.float32),
    )
    seg_wire = segments.astype(jnp.bfloat16)
    reach_devs = min(cycle_size - 1, cycle_size // 2 + 1)
    result = attend(initial, (keys, values, seg_wire), cycle_index * tok_rows, True)

    def step_back(distance, loop_state):
        kv_block, carried = loop_state
        kv_block = shifted((kv_block[0], kv_block[1], kv_block[2]), "seq", 1)
        carried = attend(
            carried, kv_block, (cycle_index - distance) * tok_rows, cycle_index >= distance
        )
        return (kv_block, carried)

    unused_block, result = lax.fori_loop(
        1, reach_devs + 1, step_back, ((keys, values, seg_wire), result)
    )
    running_max, running_sum, weighted = result
    mixed = weighted / running_sum[..., None]
    attention = (
        jnp.transpose(mixed, (2, 0, 1, 3))
        .astype(jnp.bfloat16)
        .reshape(tok_rows, local_heads * per_group * HD)
    )
    key_heads = keys.reshape(tok_rows, local_heads, HD)
    value_heads = values.reshape(tok_rows, local_heads, HD)
    gram_local = jnp.stack(
        [
            jnp.einsum("tgd,tge->gde", key_heads, key_heads, preferred_element_type=jnp.float32),
            jnp.einsum(
                "tgd,tge->gde", value_heads, value_heads, preferred_element_type=jnp.float32
            ),
        ],
        axis=1,
    )
    basis_f32 = basis.astype(jnp.float32)
    all_tokens = tok_rows * cycle_size
    gram = lax.psum(gram_local, "seq")
    captured = project(basis_f32, gram) / all_tokens
    energy = jnp.trace(gram, axis1=2, axis2=3)
    energy_total = lax.psum(jnp.sum(energy, axis=0), "kvh")
    share = KVH * energy / energy_total[None, :]
    key_lat = jnp.einsum("tgd,gdr->tgr", key_heads, basis[:, 0], preferred_element_type=jnp.float32)
    value_lat = jnp.einsum(
        "tgd,gdr->tgr", value_heads, basis[:, 1], preferred_element_type=jnp.float32
    )
    latents = (
        jnp.concatenate([key_lat, value_lat], axis=-1)
        .astype(jnp.bfloat16)
        .reshape(tok_rows, local_heads * 2 * RANK)
    )
    return (attention, latents, captured, share)


def solution(mesh):
    placed = (
        P("seq", "kvh"),
        P("seq", "kvh"),
        P("seq", "kvh"),
        P("seq"),
        P("kvh", None, None, None),
    )
    return jax.shard_map(
        body,
        mesh=mesh,
        in_specs=placed,
        out_specs=(P("seq", "kvh"), P("seq", "kvh"), P("kvh", None, None, None), P("kvh", None)),
        check_vma=False,
    )
```

profile of v0, /device:TPU:0, one launch (start us, length us, event | category | flops | bytes accessed | tf_op | source)
XLA Modules:
  0.0 101.2 jit_solution(809155110595978011)
XLA Ops:
  7.2 1.1 %convolution_bitcast_fusion = f32[2,1,128,128]{3,2,0,1:T(8,128)S(1)} fusion(bf16[128,256]{1,0:T(8,128)(2,1)} %param.9), kind=kOutput, calls=%fused_computation.21 | convolution fusion | flops 8388608 | bytes 196608 | tf_op jit(solution)/shard_map/tgd,tge->gde/dot_general | solution.py:115
  13.8 68.0 %while.44 = (s32[]{:T(128)}, bf16[128,256]{0,1:T(8,128)(2,1)S(1)}, bf16[128,256]{0,1:T(8,128)(2,1)S(1)}, bf16[128]{0:T(256)(128)(2,1)S(1)}, f32[2,8,128]{2,1,0:T...) while((s32[]{:T(128)}, bf16[128,256]{0,1:T(8,128)(2,1)S(1)}, ...), condition=%wide.region_5.6_spmd.clone, body=%wide.region_2.5_spmd.clone.sunk | while | flops 137171328 | bytes 6886943 | solution.py:100
  13.8 4.9 %collective-permute-start.2 = (bf16[128]{0:T(256)(128)(2,1)S(1)}, bf16[128]{0:T(256)(128)(2,1)S(1)}, u32[]{:S(2)}, u32[]{:S(2)}) collective-permute-start(bf16[128]{0:T(256)(128)(2,1)S(1)} %get-tuple-element.476), channel_id=1, source_target_pairs={{0,4},{4,8},{8,12},{12,16},{16,20},{20,24},{24,28},{1,5},{5,9},{9,... | collective-permute-start | bytes 776 | tf_op jit(solution)/shard_map/while/body/eval_jaxpr/ppermute | solution.py:15
  18.7 3.4 %collective-permute-start = (bf16[128,256]{0,1:T(8,128)(2,1)S(1)}, bf16[128,256]{0,1:T(8,128)(2,1)S(1)}, u32[]{:S(2)}, u32[]{:S(2)}) collective-permute-start(bf16[128,256]{0,1:T(8,128)(2,1)S(1)} %get-tuple-element.474), channel_id=1, source_target_pairs={{0,4},{4,8},{8,12},{12,16},{16,20},{20,24},{24,28},{1,5},{5,9},{9,... | collective-permute-start | bytes 196616 | tf_op jit(solution)/shard_map/while/body/eval_jaxpr/ppermute | solution.py:15
  22.1 3.4 %collective-permute-start.1 = (bf16[128,256]{0,1:T(8,128)(2,1)S(1)}, bf16[128,256]{0,1:T(8,128)(2,1)S(1)}, u32[]{:S(2)}, u32[]{:S(2)}) collective-permute-start(bf16[128,256]{0,1:T(8,128)(2,1)S(1)} %get-tuple-element.475), channel_id=1, source_target_pairs={{0,4},{4,8},{8,12},{12,16},{16,20},{20,24},{24,28},{1,5},{5,9},{9,... | collective-permute-start | bytes 196616 | tf_op jit(solution)/shard_map/while/body/eval_jaxpr/ppermute | solution.py:15
  26.4 1.1 %collective-permute-done.1 = bf16[128,256]{0,1:T(8,128)(2,1)S(1)} collective-permute-done((bf16[128,256]{0,1:T(8,128)(2,1)S(1)}, bf16[128,256]{0,1:T(8,128)(2,1)S(1)}, u32[]{:S(2)}, u32[]{:S(2)}) %collective-permute-start.1) | collective-permute-done | bytes 65568 | tf_op jit(solution)/shard_map/while/body/eval_jaxpr/ppermute | solution.py:15
  28.2 4.3 %collective-permute-start.2 = (bf16[128]{0:T(256)(128)(2,1)S(1)}, bf16[128]{0:T(256)(128)(2,1)S(1)}, u32[]{:S(2)}, u32[]{:S(2)}) collective-permute-start(bf16[128]{0:T(256)(128)(2,1)S(1)} %get-tuple-element.476), channel_id=1, source_target_pairs={{0,4},{4,8},{8,12},{12,16},{16,20},{20,24},{24,28},{1,5},{5,9},{9,... | collective-permute-start | bytes 776 | tf_op jit(solution)/shard_map/while/body/eval_jaxpr/ppermute | solution.py:15
  32.5 4.5 %collective-permute-start = (bf16[128,256]{0,1:T(8,128)(2,1)S(1)}, bf16[128,256]{0,1:T(8,128)(2,1)S(1)}, u32[]{:S(2)}, u32[]{:S(2)}) collective-permute-start(bf16[128,256]{0,1:T(8,128)(2,1)S(1)} %get-tuple-element.474), channel_id=1, source_target_pairs={{0,4},{4,8},{8,12},{12,16},{16,20},{20,24},{24,28},{1,5},{5,9},{9,... | collective-permute-start | bytes 196616 | tf_op jit(solution)/shard_map/while/body/eval_jaxpr/ppermute | solution.py:15
  36.9 2.4 %collective-permute-start.1 = (bf16[128,256]{0,1:T(8,128)(2,1)S(1)}, bf16[128,256]{0,1:T(8,128)(2,1)S(1)}, u32[]{:S(2)}, u32[]{:S(2)}) collective-permute-start(bf16[128,256]{0,1:T(8,128)(2,1)S(1)} %get-tuple-element.475), channel_id=1, source_target_pairs={{0,4},{4,8},{8,12},{12,16},{16,20},{20,24},{24,28},{1,5},{5,9},{9,... | collective-permute-start | bytes 196616 | tf_op jit(solution)/shard_map/while/body/eval_jaxpr/ppermute | solution.py:15
  40.1 1.1 %collective-permute-done.1 = bf16[128,256]{0,1:T(8,128)(2,1)S(1)} collective-permute-done((bf16[128,256]{0,1:T(8,128)(2,1)S(1)}, bf16[128,256]{0,1:T(8,128)(2,1)S(1)}, u32[]{:S(2)}, u32[]{:S(2)}) %collective-permute-start.1) | collective-permute-done | bytes 65568 | tf_op jit(solution)/shard_map/while/body/eval_jaxpr/ppermute | solution.py:15
  41.9 4.5 %collective-permute-start.2 = (bf16[128]{0:T(256)(128)(2,1)S(1)}, bf16[128]{0:T(256)(128)(2,1)S(1)}, u32[]{:S(2)}, u32[]{:S(2)}) collective-permute-start(bf16[128]{0:T(256)(128)(2,1)S(1)} %get-tuple-element.476), channel_id=1, source_target_pairs={{0,4},{4,8},{8,12},{12,16},{16,20},{20,24},{24,28},{1,5},{5,9},{9,... | collective-permute-start | bytes 776 | tf_op jit(solution)/shard_map/while/body/eval_jaxpr/ppermute | solution.py:15
  46.4 5.3 %collective-permute-start = (bf16[128,256]{0,1:T(8,128)(2,1)S(1)}, bf16[128,256]{0,1:T(8,128)(2,1)S(1)}, u32[]{:S(2)}, u32[]{:S(2)}) collective-permute-start(bf16[128,256]{0,1:T(8,128)(2,1)S(1)} %get-tuple-element.474), channel_id=1, source_target_pairs={{0,4},{4,8},{8,12},{12,16},{16,20},{20,24},{24,28},{1,5},{5,9},{9,... | collective-permute-start | bytes 196616 | tf_op jit(solution)/shard_map/while/body/eval_jaxpr/ppermute | solution.py:15
  51.7 1.9 %collective-permute-start.1 = (bf16[128,256]{0,1:T(8,128)(2,1)S(1)}, bf16[128,256]{0,1:T(8,128)(2,1)S(1)}, u32[]{:S(2)}, u32[]{:S(2)}) collective-permute-start(bf16[128,256]{0,1:T(8,128)(2,1)S(1)} %get-tuple-element.475), channel_id=1, source_target_pairs={{0,4},{4,8},{8,12},{12,16},{16,20},{20,24},{24,28},{1,5},{5,9},{9,... | collective-permute-start | bytes 196616 | tf_op jit(solution)/shard_map/while/body/eval_jaxpr/ppermute | solution.py:15
  54.4 1.1 %collective-permute-done.1 = bf16[128,256]{0,1:T(8,128)(2,1)S(1)} collective-permute-done((bf16[128,256]{0,1:T(8,128)(2,1)S(1)}, bf16[128,256]{0,1:T(8,128)(2,1)S(1)}, u32[]{:S(2)}, u32[]{:S(2)}) %collective-permute-start.1) | collective-permute-done | bytes 65568 | tf_op jit(solution)/shard_map/while/body/eval_jaxpr/ppermute | solution.py:15
  56.2 4.4 %collective-permute-start.2 = (bf16[128]{0:T(256)(128)(2,1)S(1)}, bf16[128]{0:T(256)(128)(2,1)S(1)}, u32[]{:S(2)}, u32[]{:S(2)}) collective-permute-start(bf16[128]{0:T(256)(128)(2,1)S(1)} %get-tuple-element.476), channel_id=1, source_target_pairs={{0,4},{4,8},{8,12},{12,16},{16,20},{20,24},{24,28},{1,5},{5,9},{9,... | collective-permute-start | bytes 776 | tf_op jit(solution)/shard_map/while/body/eval_jaxpr/ppermute | solution.py:15
  60.6 5.0 %collective-permute-start = (bf16[128,256]{0,1:T(8,128)(2,1)S(1)}, bf16[128,256]{0,1:T(8,128)(2,1)S(1)}, u32[]{:S(2)}, u32[]{:S(2)}) collective-permute-start(bf16[128,256]{0,1:T(8,128)(2,1)S(1)} %get-tuple-element.474), channel_id=1, source_target_pairs={{0,4},{4,8},{8,12},{12,16},{16,20},{20,24},{24,28},{1,5},{5,9},{9,... | collective-permute-start | bytes 196616 | tf_op jit(solution)/shard_map/while/body/eval_jaxpr/ppermute | solution.py:15
  65.6 1.9 %collective-permute-start.1 = (bf16[128,256]{0,1:T(8,128)(2,1)S(1)}, bf16[128,256]{0,1:T(8,128)(2,1)S(1)}, u32[]{:S(2)}, u32[]{:S(2)}) collective-permute-start(bf16[128,256]{0,1:T(8,128)(2,1)S(1)} %get-tuple-element.475), channel_id=1, source_target_pairs={{0,4},{4,8},{8,12},{12,16},{16,20},{20,24},{24,28},{1,5},{5,9},{9,... | collective-permute-start | bytes 196616 | tf_op jit(solution)/shard_map/while/body/eval_jaxpr/ppermute | solution.py:15
  68.3 1.1 %collective-permute-done.1 = bf16[128,256]{0,1:T(8,128)(2,1)S(1)} collective-permute-done((bf16[128,256]{0,1:T(8,128)(2,1)S(1)}, bf16[128,256]{0,1:T(8,128)(2,1)S(1)}, u32[]{:S(2)}, u32[]{:S(2)}) %collective-permute-start.1) | collective-permute-done | bytes 65568 | tf_op jit(solution)/shard_map/while/body/eval_jaxpr/ppermute | solution.py:15
  70.1 4.3 %collective-permute-start.2 = (bf16[128]{0:T(256)(128)(2,1)S(1)}, bf16[128]{0:T(256)(128)(2,1)S(1)}, u32[]{:S(2)}, u32[]{:S(2)}) collective-permute-start(bf16[128]{0:T(256)(128)(2,1)S(1)} %get-tuple-element.476), channel_id=1, source_target_pairs={{0,4},{4,8},{8,12},{12,16},{16,20},{20,24},{24,28},{1,5},{5,9},{9,... | collective-permute-start | bytes 776 | tf_op jit(solution)/shard_map/while/body/eval_jaxpr/ppermute | solution.py:15
  74.4 2.8 %collective-permute-start = (bf16[128,256]{0,1:T(8,128)(2,1)S(1)}, bf16[128,256]{0,1:T(8,128)(2,1)S(1)}, u32[]{:S(2)}, u32[]{:S(2)}) collective-permute-start(bf16[128,256]{0,1:T(8,128)(2,1)S(1)} %get-tuple-element.474), channel_id=1, source_target_pairs={{0,4},{4,8},{8,12},{12,16},{16,20},{20,24},{24,28},{1,5},{5,9},{9,... | collective-permute-start | bytes 196616 | tf_op jit(solution)/shard_map/while/body/eval_jaxpr/ppermute | solution.py:15
  77.2 1.9 %collective-permute-start.1 = (bf16[128,256]{0,1:T(8,128)(2,1)S(1)}, bf16[128,256]{0,1:T(8,128)(2,1)S(1)}, u32[]{:S(2)}, u32[]{:S(2)}) collective-permute-start(bf16[128,256]{0,1:T(8,128)(2,1)S(1)} %get-tuple-element.475), channel_id=1, source_target_pairs={{0,4},{4,8},{8,12},{12,16},{16,20},{20,24},{24,28},{1,5},{5,9},{9,... | collective-permute-start | bytes 196616 | tf_op jit(solution)/shard_map/while/body/eval_jaxpr/ppermute | solution.py:15
  84.3 1.4 %all-reduce.2.cloned.1.call-done = f32[2,2,128,128]{3,2,0,1:T(8,128)} async-done(((f32[2,2,128,128]{3,2,0,1:T(8,128)}), f32[2,2,128,128]{3,2,0,1:T(8,128)}) %all-reduce.2.cloned.1.call-update) | async-done | bytes 262160 | tf_op jit(solution)/shard_map/psum | solution.py:123
  85.7 1.2 %select_reduce_fusion = (f32[2]{0:T(128)S(1)}, f32[2,2]{0,1:T(2,128)S(1)}) fusion(f32[2,2,128,128]{3,2,0,1:T(8,128)} %all-reduce.2.cloned.1.call-done, pred[128,128]{1,0:T(8,128)(4,1)S(1)} %iota_compare_fusion), kind=kLoop, calls=%fused_computation.40 | loop fusion | flops 196602 | bytes 278552 | tf_op jit(solution)/shard_map/reduce_sum | solution.py:126
  86.9 5.7 %psum.15 = f32[2]{0:T(128)S(1)} all-reduce(f32[2]{0:T(128)S(1)} %get-tuple-element.343), channel_id=1, replica_groups=mesh['seq'=8,'kvh'=4] {'kvh'}, use_global_device_ids=true, to_apply=%region_9.10 | all-reduce | flops 2 | bytes 16 | tf_op jit(solution)/shard_map/psum | solution.py:126
  (112 shorter events, 17.7 us)
Async XLA Ops:
  7.2 1.2 %copy-start = (bf16[128,256]{1,0:T(8,128)(2,1)S(1)}, bf16[128,256]{1,0:T(8,128)(2,1)}, u32[]{:S(2)}) copy-start(bf16[128,256]{1,0:T(8,128)(2,1)} %param.8) | copy-start | bytes 196612
  7.2 78.5 %all-reduce.2.cloned.1.call-start = ((), (), s32[]{:S(2)}) async-start(), calls=%async_computation | async-start | bytes 524288 | tf_op jit(solution)/shard_map/psum | solution.py:123
  8.6 1.9 %copy-start.3 = (bf16[128,2048]{1,0:T(8,128)(2,1)S(1)}, bf16[128,2048]{1,0:T(8,128)(2,1)}, u32[]{:S(2)}) copy-start(bf16[128,2048]{1,0:T(8,128)(2,1)} %param.7) | copy-start | bytes 1572868
  9.3 0.8 copy-start.1
  11.0 0.7 copy-start.5
  12.3 0.8 copy-start.4
  13.8 11.8 %collective-permute-start.2 = (bf16[128]{0:T(256)(128)(2,1)S(1)}, bf16[128]{0:T(256)(128)(2,1)S(1)}, u32[]{:S(2)}, u32[]{:S(2)}) collective-permute-start(bf16[128]{0:T(256)(128)(2,1)S(1)} %get-tuple-element.476), channel_id=1, source_target_pairs={{0,4},{4,8},{8,12},{12,16},{16,20},{20,24},{24,28},{1,5},{5,9},{9,... | collective-permute-start | bytes 776 | tf_op jit(solution)/shard_map/while/body/eval_jaxpr/ppermute | solution.py:15
  18.7 7.0 %collective-permute-start = (bf16[128,256]{0,1:T(8,128)(2,1)S(1)}, bf16[128,256]{0,1:T(8,128)(2,1)S(1)}, u32[]{:S(2)}, u32[]{:S(2)}) collective-permute-start(bf16[128,256]{0,1:T(8,128)(2,1)S(1)} %get-tuple-element.474), channel_id=1, source_target_pairs={{0,4},{4,8},{8,12},{12,16},{16,20},{20,24},{24,28},{1,5},{5,9},{9,... | collective-permute-start | bytes 196616 | tf_op jit(solution)/shard_map/while/body/eval_jaxpr/ppermute | solution.py:15
  22.1 5.3 %collective-permute-start.1 = (bf16[128,256]{0,1:T(8,128)(2,1)S(1)}, bf16[128,256]{0,1:T(8,128)(2,1)S(1)}, u32[]{:S(2)}, u32[]{:S(2)}) collective-permute-start(bf16[128,256]{0,1:T(8,128)(2,1)S(1)} %get-tuple-element.475), channel_id=1, source_target_pairs={{0,4},{4,8},{8,12},{12,16},{16,20},{20,24},{24,28},{1,5},{5,9},{9,... | collective-permute-start | bytes 196616 | tf_op jit(solution)/shard_map/while/body/eval_jaxpr/ppermute | solution.py:15
  28.2 11.2 %collective-permute-start.2 = (bf16[128]{0:T(256)(128)(2,1)S(1)}, bf16[128]{0:T(256)(128)(2,1)S(1)}, u32[]{:S(2)}, u32[]{:S(2)}) collective-permute-start(bf16[128]{0:T(256)(128)(2,1)S(1)} %get-tuple-element.476), channel_id=1, source_target_pairs={{0,4},{4,8},{8,12},{12,16},{16,20},{20,24},{24,28},{1,5},{5,9},{9,... | collective-permute-start | bytes 776 | tf_op jit(solution)/shard_map/while/body/eval_jaxpr/ppermute | solution.py:15
  32.5 7.0 %collective-permute-start = (bf16[128,256]{0,1:T(8,128)(2,1)S(1)}, bf16[128,256]{0,1:T(8,128)(2,1)S(1)}, u32[]{:S(2)}, u32[]{:S(2)}) collective-permute-start(bf16[128,256]{0,1:T(8,128)(2,1)S(1)} %get-tuple-element.474), channel_id=1, source_target_pairs={{0,4},{4,8},{8,12},{12,16},{16,20},{20,24},{24,28},{1,5},{5,9},{9,... | collective-permute-start | bytes 196616 | tf_op jit(solution)/shard_map/while/body/eval_jaxpr/ppermute | solution.py:15
  36.9 4.3 %collective-permute-start.1 = (bf16[128,256]{0,1:T(8,128)(2,1)S(1)}, bf16[128,256]{0,1:T(8,128)(2,1)S(1)}, u32[]{:S(2)}, u32[]{:S(2)}) collective-permute-start(bf16[128,256]{0,1:T(8,128)(2,1)S(1)} %get-tuple-element.475), channel_id=1, source_target_pairs={{0,4},{4,8},{8,12},{12,16},{16,20},{20,24},{24,28},{1,5},{5,9},{9,... | collective-permute-start | bytes 196616 | tf_op jit(solution)/shard_map/while/body/eval_jaxpr/ppermute | solution.py:15
  41.9 11.7 %collective-permute-start.2 = (bf16[128]{0:T(256)(128)(2,1)S(1)}, bf16[128]{0:T(256)(128)(2,1)S(1)}, u32[]{:S(2)}, u32[]{:S(2)}) collective-permute-start(bf16[128]{0:T(256)(128)(2,1)S(1)} %get-tuple-element.476), channel_id=1, source_target_pairs={{0,4},{4,8},{8,12},{12,16},{16,20},{20,24},{24,28},{1,5},{5,9},{9,... | collective-permute-start | bytes 776 | tf_op jit(solution)/shard_map/while/body/eval_jaxpr/ppermute | solution.py:15
  46.4 7.4 %collective-permute-start = (bf16[128,256]{0,1:T(8,128)(2,1)S(1)}, bf16[128,256]{0,1:T(8,128)(2,1)S(1)}, u32[]{:S(2)}, u32[]{:S(2)}) collective-permute-start(bf16[128,256]{0,1:T(8,128)(2,1)S(1)} %get-tuple-element.474), channel_id=1, source_target_pairs={{0,4},{4,8},{8,12},{12,16},{16,20},{20,24},{24,28},{1,5},{5,9},{9,... | collective-permute-start | bytes 196616 | tf_op jit(solution)/shard_map/while/body/eval_jaxpr/ppermute | solution.py:15
  51.7 3.8 %collective-permute-start.1 = (bf16[128,256]{0,1:T(8,128)(2,1)S(1)}, bf16[128,256]{0,1:T(8,128)(2,1)S(1)}, u32[]{:S(2)}, u32[]{:S(2)}) collective-permute-start(bf16[128,256]{0,1:T(8,128)(2,1)S(1)} %get-tuple-element.475), channel_id=1, source_target_pairs={{0,4},{4,8},{8,12},{12,16},{16,20},{20,24},{24,28},{1,5},{5,9},{9,... | collective-permute-start | bytes 196616 | tf_op jit(solution)/shard_map/while/body/eval_jaxpr/ppermute | solution.py:15
  56.2 11.3 %collective-permute-start.2 = (bf16[128]{0:T(256)(128)(2,1)S(1)}, bf16[128]{0:T(256)(128)(2,1)S(1)}, u32[]{:S(2)}, u32[]{:S(2)}) collective-permute-start(bf16[128]{0:T(256)(128)(2,1)S(1)} %get-tuple-element.476), channel_id=1, source_target_pairs={{0,4},{4,8},{8,12},{12,16},{16,20},{20,24},{24,28},{1,5},{5,9},{9,... | collective-permute-start | bytes 776 | tf_op jit(solution)/shard_map/while/body/eval_jaxpr/ppermute | solution.py:15
  60.6 7.1 %collective-permute-start = (bf16[128,256]{0,1:T(8,128)(2,1)S(1)}, bf16[128,256]{0,1:T(8,128)(2,1)S(1)}, u32[]{:S(2)}, u32[]{:S(2)}) collective-permute-start(bf16[128,256]{0,1:T(8,128)(2,1)S(1)} %get-tuple-element.474), channel_id=1, source_target_pairs={{0,4},{4,8},{8,12},{12,16},{16,20},{20,24},{24,28},{1,5},{5,9},{9,... | collective-permute-start | bytes 196616 | tf_op jit(solution)/shard_map/while/body/eval_jaxpr/ppermute | solution.py:15
  65.6 3.8 %collective-permute-start.1 = (bf16[128,256]{0,1:T(8,128)(2,1)S(1)}, bf16[128,256]{0,1:T(8,128)(2,1)S(1)}, u32[]{:S(2)}, u32[]{:S(2)}) collective-permute-start(bf16[128,256]{0,1:T(8,128)(2,1)S(1)} %get-tuple-element.475), channel_id=1, source_target_pairs={{0,4},{4,8},{8,12},{12,16},{16,20},{20,24},{24,28},{1,5},{5,9},{9,... | collective-permute-start | bytes 196616 | tf_op jit(solution)/shard_map/while/body/eval_jaxpr/ppermute | solution.py:15
  70.1 9.1 %collective-permute-start.2 = (bf16[128]{0:T(256)(128)(2,1)S(1)}, bf16[128]{0:T(256)(128)(2,1)S(1)}, u32[]{:S(2)}, u32[]{:S(2)}) collective-permute-start(bf16[128]{0:T(256)(128)(2,1)S(1)} %get-tuple-element.476), channel_id=1, source_target_pairs={{0,4},{4,8},{8,12},{12,16},{16,20},{20,24},{24,28},{1,5},{5,9},{9,... | collective-permute-start | bytes 776 | tf_op jit(solution)/shard_map/while/body/eval_jaxpr/ppermute | solution.py:15
  74.4 4.9 %collective-permute-start = (bf16[128,256]{0,1:T(8,128)(2,1)S(1)}, bf16[128,256]{0,1:T(8,128)(2,1)S(1)}, u32[]{:S(2)}, u32[]{:S(2)}) collective-permute-start(bf16[128,256]{0,1:T(8,128)(2,1)S(1)} %get-tuple-element.474), channel_id=1, source_target_pairs={{0,4},{4,8},{8,12},{12,16},{16,20},{20,24},{24,28},{1,5},{5,9},{9,... | collective-permute-start | bytes 196616 | tf_op jit(solution)/shard_map/while/body/eval_jaxpr/ppermute | solution.py:15
  77.2 3.8 %collective-permute-start.1 = (bf16[128,256]{0,1:T(8,128)(2,1)S(1)}, bf16[128,256]{0,1:T(8,128)(2,1)S(1)}, u32[]{:S(2)}, u32[]{:S(2)}) collective-permute-start(bf16[128,256]{0,1:T(8,128)(2,1)S(1)} %get-tuple-element.475), channel_id=1, source_target_pairs={{0,4},{4,8},{8,12},{12,16},{16,20},{20,24},{24,28},{1,5},{5,9},{9,... | collective-permute-start | bytes 196616 | tf_op jit(solution)/shard_map/while/body/eval_jaxpr/ppermute | solution.py:15
  85.7 7.6 %copy-start.2 = (f32[2,2,128,128]{3,2,0,1:T(8,128)S(1)}, f32[2,2,128,128]{3,2,0,1:T(8,128)}, u32[]{:S(2)}) copy-start(f32[2,2,128,128]{3,2,0,1:T(8,128)} %all-reduce.2.cloned.1.call-done) | copy-start | bytes 786436
Sparse Core Ops, SparseCore 0:
  11.3 74.3 all-reduce.1
where the time goes:
time: 102 us; the launch traced here: 101 us
  starting transfers between devices  54.8 us (54%)
  between operations  14.2 us (14%)
  matrix products  8.75 us (9%)
  waiting for transfers between devices  6.9 us (7%)
  local copies, waits for them, and re-layouts  5.81 us (6%)
  blocking collectives  5.66 us (6%)
  other arithmetic  4.25 us (4%)
    ppermute x15, starting transfers between devices, shifted(): return lax.ppermute(block, axis, route)  54.8 us
    psum x1, blocking collectives, body(): energy_total = lax.psum(jnp.sum(energy, axis=0), 'kvh')  5.66 us
    ppermute x15, waiting for transfers between devices, shifted(): return lax.ppermute(block, axis, route)  5.48 us
    unnamed x19, local copies, waits for them, and re-layouts  5.31 us
    dot_general x6, matrix products, one_part(): jnp.einsum('gjts,sgd->gjtd', weights.astype(jnp.bfloat16), value_part, pr...  3.96 us
    dot_general x6, matrix products, one_part(): jnp.einsum('tgjd,sgd->gjts', query_heads, key_part, preferred_element_typ...  2.14 us
  transfers between devices with their start and end apart: 16, of which 6 were waited for; matrix products, arithmetic and copies ran while one was open for 11% of the time, Pallas kernels for 0%

commit v1 on v0

v1 whole, which is shorter than its diff:
```python
import functools
import math

import jax
import jax.numpy as jnp
from jax import lax
from jax.experimental import pallas as pl
from jax.experimental.pallas import tpu as pltpu
from jax.sharding import PartitionSpec as P

MESH = pl.DeviceIdType.MESH
NEG = -1e30


def remote(src, dst, send, recv, device):
    return pltpu.make_async_remote_copy(
        src_ref=src, dst_ref=dst, send_sem=send, recv_sem=recv, device_id=device, device_id_type=MESH
    )


def kernel(
    n, kv_n, reach, heads, group, hd, rank,
    q_hbm, k_hbm, v_hbm, seg_hbm, basis_hbm,
    att_hbm, lat_ref, cap_ref, share_ref,
    qbuf, qt, kbuf, vbuf, segbuf, basis, vt, bias, mx, sums, acc, outv, latf, mine, theirs, ebuf,
    in_sem, out_sem, send_sem, recv_sem, bf_send, bf_recv, e_send, e_recv,
):
    me = lax.axis_index("seq")
    kv = lax.axis_index("kvh")
    odd = lax.rem(me, 2)
    rows = kbuf.shape[1]
    rounds = int(math.log2(n))
    scale = float(hd) ** -0.5 * math.log2(math.e)
    wide = 2 * rows
    chunks = group * rows // wide
    parts = 2 * heads

    loads = [
        pltpu.make_async_copy(src, dst, in_sem.at[i])
        for i, (src, dst) in enumerate(
            [
                (k_hbm, kbuf.at[0]),
                (v_hbm, vbuf.at[0]),
                (seg_hbm, segbuf.at[0]),
                (basis_hbm, basis),
                (q_hbm, qbuf),
            ]
        )
    ]
    for load in loads:
        load.start()

    barrier = pltpu.get_barrier_semaphore()

    def greet(condition, **where):
        @pl.when(condition)
        def _():
            pl.semaphore_signal(barrier, inc=1, device_id=where, device_id_type=MESH)

    count = 0
    for step in (-2, -1, 1, 2):
        inside = (me + step >= 0) & (me + step < n)
        greet(inside, seq=me + step)
        count = count + inside.astype(jnp.int32)

    def partner(r):
        bit = lax.rem(me // (1 << r), 2)
        return me + (1 << r) * (1 - 2 * bit)

    for r in range(2, rounds):
        pl.semaphore_signal(barrier, inc=1, device_id={"seq": partner(r)}, device_id_type=MESH)
    for o in range(1, kv_n):
        pl.semaphore_signal(
            barrier, inc=1, device_id={"kvh": lax.rem(kv + o, kv_n)}, device_id_type=MESH
        )
    pl.semaphore_wait(barrier, count + (rounds - 2) + (kv_n - 1))

    bufs = (segbuf, kbuf, vbuf)
    own = (seg_hbm, k_hbm, v_hbm)

    def routes(e):
        out = []
        if e + 2 <= reach:
            out.append((0, 2, me + 2 < n))
        if e + 1 <= reach:
            out.append((1, 1, odd == 0))
        if e >= 2:
            out.append((1, -1, odd == 1))
        if e + 1 == reach:
            out.append((2, 1, (odd == 1) & (me + 1 < n)))
        return out

    def copies(e, which):
        found = []
        for lane, step, ok in routes(e):
            src = own[which] if e == 0 else bufs[which].at[e]
            copy = remote(
                src,
                bufs[which].at[e + step],
                send_sem.at[e, lane, which],
                recv_sem.at[e + step, which],
                {"seq": me + step},
            )
            found.append((ok & (me >= e), copy))
        return found

    def send(e, which):
        for ok, copy in copies(e, which):
            pl.when(ok)(copy.start)

    def receive(d, which):
        copy = remote(
            bufs[which].at[0],
            bufs[which].at[d],
            send_sem.at[0, 0, which],
            recv_sem.at[d, which],
            {"seq": me},
        )
        pl.when(me >= d)(copy.wait_recv)

    def forward(e):
        for which in range(3):
            receive(e, which)
            send(e, which)

    for which in (1, 2, 0):
        send(0, which)

    for load in loads[:4]:
        load.wait()

    blocks = []
    for g in range(heads):
        cols = slice(g * hd, (g + 1) * hd)
        blocks += [kbuf[0, :, cols], vbuf[0, :, cols]]
    for i in range(parts):
        latf[:, i * rank : (i + 1) * rank] = jnp.dot(
            blocks[i], basis[i // 2, i % 2], preferred_element_type=jnp.float32
        )
    lat = latf[...]
    lat_ref[...] = lat.astype(lat_ref.dtype)
    products = lax.dot_general(
        lat,
        lat,
        (((0,), (0,)), ((), ())),
        precision=lax.Precision.HIGHEST,
        preferred_element_type=jnp.float32,
    )
    column = lax.broadcasted_iota(jnp.int32, (rank, parts * rank), 1) // rank
    seen = jnp.zeros((rank, parts * rank), jnp.float32)
    for i in range(parts):
        seen = jnp.where(column == i, products[i * rank : (i + 1) * rank, :], seen)
    mine[0, :rank, :] = seen
    row = lax.broadcasted_iota(jnp.int32, (8, hd), 0)
    squares = jnp.zeros((8, hd), jnp.float32)
    for i in range(parts):
        block = blocks[i].astype(jnp.float32)
        squares = jnp.where(row == i, jnp.sum(block * block, axis=0, keepdims=True), squares)
    mine[0, rank:, :] = squares

    def butterfly(r):
        return remote(mine.at[r], theirs.at[r], bf_send.at[r], bf_recv.at[r], {"seq": partner(r)})

    def spread(o):
        return remote(
            mine.at[rounds, pl.ds(rank, 8)],
            ebuf.at[o],
            e_send.at[o],
            e_recv.at[o],
            {"kvh": lax.rem(kv + o, kv_n)},
        )

    def finish():
        for o in range(1, kv_n):
            spread(o).wait()
        energy = mine[rounds, rank:, :]
        total = energy
        for o in range(1, kv_n):
            total = total + ebuf[o]
        energy = jnp.sum(energy, axis=1, keepdims=True)
        total = jnp.sum(total, axis=1, keepdims=True)
        for c in range(2):
            whole = total[c : c + 1]
            for g in range(1, heads):
                whole = whole + total[2 * g + c : 2 * g + c + 1]
            for g in range(heads):
                i = 2 * g + c
                share_ref[g : g + 1, c : c + 1] = (heads * kv_n) * energy[i : i + 1] / whole
        for i in range(parts):
            cap_ref[i // 2, i % 2] = mine[rounds, :rank, i * rank : (i + 1) * rank] / (rows * n)

    stage = [0]

    def advance():
        r = stage[0]
        stage[0] += 1
        if r < rounds:
            butterfly(r).wait()
            mine[r + 1] = mine[r] + theirs[r]
            if r + 1 < rounds:
                butterfly(r + 1).start()
            else:
                for o in range(1, kv_n):
                    spread(o).start()
        elif r == rounds:
            finish()

    butterfly(0).start()
    loads[4].wait()

    def turn(h, carry):
        at = pl.ds(pl.multiple_of(h * hd, hd), hd)
        to = pl.ds(pl.multiple_of(h * rows, rows), rows)
        qt[:, to] = qbuf[:, at].T
        return carry

    lax.fori_loop(0, heads * group, turn, 0)

    def attend(d):
        def work():
            seg_q = jnp.broadcast_to(segbuf[0].astype(jnp.float32), (rows, rows))
            seg_k = jnp.broadcast_to(segbuf[d].astype(jnp.float32), (rows, rows)).T
            allowed = seg_q == seg_k
            if d == 0:
                allowed = allowed & (
                    lax.broadcasted_iota(jnp.int32, (rows, rows), 0)
                    <= lax.broadcasted_iota(jnp.int32, (rows, rows), 1)
                )
            hidden = jnp.where(allowed, 0.0, NEG)
            bias[:, :rows] = hidden
            bias[:, rows:] = hidden
            for g in range(heads):
                vt[g] = vbuf[d, :, g * hd : (g + 1) * hd].T

            for g in range(heads):

                def one(c, carry, g=g):
                    at = pl.ds(pl.multiple_of(g * group * rows + c * wide, wide), wide)
                    scores = jnp.dot(
                        kbuf[d, :, g * hd : (g + 1) * hd],
                        qt[:, at],
                        preferred_element_type=jnp.float32,
                    )
                    scores = scores + bias[...]
                    top = jnp.max(scores, axis=0, keepdims=True)
                    if d > 0:
                        before = mx[:, at]
                        top = jnp.maximum(top, before)
                    weights = jnp.exp2((scores - top) * scale)
                    added = jnp.sum(weights, axis=0, keepdims=True)
                    mixed = jnp.dot(
                        vt[g], weights.astype(jnp.bfloat16), preferred_element_type=jnp.float32
                    )
                    if d > 0:
                        factor = jnp.exp2((before - top) * scale)
                        added = added + sums[:, at] * factor
                        mixed = mixed + acc[:, at] * factor
                    mx[:, at] = top
                    sums[:, at] = added
                    acc[:, at] = mixed
                    return carry

                lax.fori_loop(0, chunks, one, 0)

        if d == 0:
            work()
        else:

            @pl.when(me >= d)
            def _():
                if d % 2 == 1:
                    for which in range(3):
                        receive(d, which)
                work()

    attend(0)
    for e in range(2, reach + 1, 2):
        forward(e)
        advance()
        if e >= 4:
            attend(e - 3)
        attend(e)
        advance()
    last_even = reach - reach % 2
    if last_even >= 2:
        attend(last_even - 1)
    while stage[0] <= rounds:
        advance()
    if reach > last_even:
        attend(reach)

    def settle(h, carry):
        at = pl.ds(pl.multiple_of(h * rows, rows), rows)
        to = pl.ds(pl.multiple_of(h * hd, hd), hd)
        mixed = acc[:, at] * (1.0 / sums[:, at])
        outv[:, to] = mixed.T.astype(outv.dtype)
        return carry

    lax.fori_loop(0, heads * group, settle, 0)
    store = pltpu.make_async_copy(outv, att_hbm, out_sem)
    store.start()
    for e in range(0, reach + 1, 2):
        for which in range(3):
            for ok, copy in copies(e, which):
                pl.when(ok)(copy.wait_send)
    store.wait()


def body(n, kv_n, queries, keys, values, segments, basis):
    rows = queries.shape[0]
    heads, _, hd, rank = basis.shape
    group = queries.shape[1] // (heads * hd)
    reach = min(n - 1, n // 2 + 1)
    rounds = int(math.log2(n))
    width = heads * hd
    lanes = heads * group * rows
    f32, bf16 = jnp.float32, jnp.bfloat16
    dma = pltpu.SemaphoreType.DMA
    any_space = pl.BlockSpec(memory_space=pl.ANY)
    vmem = pl.BlockSpec(memory_space=pltpu.VMEM)
    return pl.pallas_call(
        functools.partial(kernel, n, kv_n, reach, heads, group, hd, rank),
        out_shape=(
            jax.ShapeDtypeStruct(queries.shape, bf16),
            jax.ShapeDtypeStruct((rows, heads * 2 * rank), bf16),
            jax.ShapeDtypeStruct((heads, 2, rank, rank), f32),
            jax.ShapeDtypeStruct((heads, 2), f32),
        ),
        in_specs=[any_space] * 5,
        out_specs=(any_space, vmem, vmem, vmem),
        scratch_shapes=[
            pltpu.VMEM(queries.shape, bf16),
            pltpu.VMEM((hd, lanes), bf16),
            pltpu.VMEM((reach + 1, rows, width), bf16),
            pltpu.VMEM((reach + 1, rows, width), bf16),
            pltpu.VMEM((reach + 1, 1, rows), jnp.int32),
            pltpu.VMEM(basis.shape, bf16),
            pltpu.VMEM((heads, hd, rows), bf16),
            pltpu.VMEM((rows, 2 * rows), f32),
            pltpu.VMEM((1, lanes), f32),
            pltpu.VMEM((1, lanes), f32),
            pltpu.VMEM((hd, lanes), f32),
            pltpu.VMEM(queries.shape, bf16),
            pltpu.VMEM((rows, 2 * heads * rank), f32),
            pltpu.VMEM((rounds + 1, rank + 8, hd), f32),
            pltpu.VMEM((rounds, rank + 8, hd), f32),
            pltpu.VMEM((kv_n, 8, hd), f32),
            dma((5,)),
            dma,
            dma((reach + 1, 3, 3)),
            dma((reach + 1, 3)),
            dma((rounds,)),
            dma((rounds,)),
            dma((kv_n,)),
            dma((kv_n,)),
        ],
        compiler_params=pltpu.CompilerParams(collective_id=0, has_side_effects=True),
    )(queries, keys, values, segments.reshape(1, rows), basis)


def solution(mesh):
    placed = (
        P("seq", "kvh"),
        P("seq", "kvh"),
        P("seq", "kvh"),
        P("seq"),
        P("kvh", None, None, None),
    )
    return jax.shard_map(
        functools.partial(body, mesh.shape["seq"], mesh.shape["kvh"]),
        mesh=mesh,
        in_specs=placed,
        out_specs=(P("seq", "kvh"), P("seq", "kvh"), P("kvh", None, None, None), P("kvh", None)),
        check_vma=False,
    )
```

time: 102 us -> 35.4 us (0.35)
  the two profiles are of different devices: /device:TPU:0 before, /device:TPU:20 now
where the time goes in v1:
time: 35.4 us; the launch traced here: 35.1 us
  Pallas kernels  29 us (82%)
  local copies, waits for them, and re-layouts  5.45 us (15%)
  between operations  0.65 us (2%)
    pallas_call x1, Pallas kernels, body(): pl.pallas_call(functools.partial(kernel, n, kv_n, reach, heads, group, hd...  29 us
    unnamed x11, local copies, waits for them, and re-layouts  5.45 us

profile of v1, /device:TPU:20, one launch (start us, length us, event | category | flops | bytes accessed | tf_op | source)
XLA Modules:
  0.0 35.1 jit_solution(14977920250593945806)
XLA Ops:
  0.6 1.5 %copy.9.basis_hbm = bf16[2,2,128,32]{3,2,1,0:T(8,128)(2,1)} copy(bf16[2,2,128,32]{2,3,1,0:T(8,128)(2,1)} %param.9) | data formatting | bytes 65536 | tf_op args[4]
  2.1 29.0 %shard_map.84 = (bf16[128,2048]{1,0:T(8,128)(2,1)}, bf16[128,128]{1,0:T(8,128)(2,1)}, f32[2,2,32,32]{3,2,1,0:T(8,128)}, f32[2,2]{1,0:T(2,128)}) custom-call(bf16[128,2048]{1,0:T(8,128)(2,1)} %q_hbm.1, bf16[128,256]{1,0:T(8,128)(2,1)} %k_hbm.1, bf16[128,256]{1,0:T(8,128)(2,1)} %v_hbm.1, s32[1,128]{1,0:T(1,128)} %bitcast.1, bf16[2,2,128,32]{3,2,1,0:T(8,128)(2,1)} %copy.9.basis_hbm), custom_call_target="tpu_custom_call" | custom-call | tf_op jit(solution)/shard_map/pallas_call | solution.py:321
  31.1 0.0 copy-start.1
  31.1 1.9 %copy.14 = bf16[128,2048]{1,0:T(8,128)(2,1)} copy(bf16[128,2048]{1,0:T(8,128)(2,1)} %get-tuple-element.8) | data formatting | bytes 1048576
  33.0 0.0 copy-done.1
  33.0 0.0 copy-start
  33.0 0.6 %copy.15 = bf16[128,128]{1,0:T(8,128)(2,1)} copy(bf16[128,128]{1,0:T(8,128)(2,1)S(1)} %copy-done.1) | data formatting | bytes 65536
  33.7 0.2 copy-done
  33.9 0.0 copy-start.2
  33.9 0.6 %copy.16 = f32[2,2,32,32]{3,2,1,0:T(8,128)} copy(f32[2,2,32,32]{3,2,1,0:T(8,128)S(1)} %copy-done) | data formatting | bytes 32768
  34.5 0.0 copy-done.2
  34.5 0.6 %copy.17 = f32[2,2]{1,0:T(2,128)} copy(f32[2,2]{1,0:T(2,128)S(1)} %copy-done.2) | data formatting | bytes 32
Async XLA Ops:
  31.1 1.9 %copy-start.1 = (bf16[128,128]{1,0:T(8,128)(2,1)S(1)}, bf16[128,128]{1,0:T(8,128)(2,1)}, u32[]{:S(2)}) copy-start(bf16[128,128]{1,0:T(8,128)(2,1)} %get-tuple-element.9) | copy-start | bytes 98308
  33.0 0.9 %copy-start = (f32[2,2,32,32]{3,2,1,0:T(8,128)S(1)}, f32[2,2,32,32]{3,2,1,0:T(8,128)}, u32[]{:S(2)}) copy-start(f32[2,2,32,32]{3,2,1,0:T(8,128)} %get-tuple-element.10) | copy-start | bytes 49156
  33.9 0.6 %copy-start.2 = (f32[2,2]{1,0:T(2,128)S(1)}, f32[2,2]{1,0:T(2,128)}, u32[]{:S(2)}) copy-start(f32[2,2]{1,0:T(2,128)} %get-tuple-element.11) | copy-start | bytes 52

commit v2 on v1

--- a/solution.py
+++ b/solution.py
@@ -10,6 +10,7 @@
 
 MESH = pl.DeviceIdType.MESH
 NEG = -1e30
+LIMIT = 24 << 20
 
 
 def remote(src, dst, send, recv, device):
@@ -21,9 +22,9 @@
 def kernel(
     n, kv_n, reach, heads, group, hd, rank,
     q_hbm, k_hbm, v_hbm, seg_hbm, basis_hbm,
-    att_hbm, lat_ref, cap_ref, share_ref,
-    qbuf, qt, kbuf, vbuf, segbuf, basis, vt, bias, mx, sums, acc, outv, latf, mine, theirs, ebuf,
-    in_sem, out_sem, send_sem, recv_sem, bf_send, bf_recv, e_send, e_recv,
+    att_ref, lat_ref, cap_ref, share_ref,
+    qbuf, qt, kbuf, vbuf, segbuf, basis, vt, bias, mx, sums, acc, latf, mine, theirs, ebuf,
+    in_sem, send_sem, recv_sem, bf_send, bf_recv, e_send, e_recv,
 ):
     me = lax.axis_index("seq")
     kv = lax.axis_index("kvh")
@@ -34,6 +35,7 @@
     wide = 2 * rows
     chunks = group * rows // wide
     parts = 2 * heads
+    unroll = reach < 8
 
     loads = [
         pltpu.make_async_copy(src, dst, in_sem.at[i])
@@ -73,6 +75,16 @@
         pl.semaphore_signal(
             barrier, inc=1, device_id={"kvh": lax.rem(kv + o, kv_n)}, device_id_type=MESH
         )
+    loads[4].wait()
+
+    def turn(h, carry):
+        at = pl.ds(pl.multiple_of(h * hd, hd), hd)
+        to = pl.ds(pl.multiple_of(h * rows, rows), rows)
+        qt[:, to] = qbuf[:, at].T
+        return carry
+
+    lax.fori_loop(0, heads * group, turn, 0, unroll=unroll)
+
     pl.semaphore_wait(barrier, count + (rounds - 2) + (kv_n - 1))
 
     bufs = (segbuf, kbuf, vbuf)
@@ -134,8 +146,11 @@
         cols = slice(g * hd, (g + 1) * hd)
         blocks += [kbuf[0, :, cols], vbuf[0, :, cols]]
     for i in range(parts):
-        latf[:, i * rank : (i + 1) * rank] = jnp.dot(
-            blocks[i], basis[i // 2, i % 2], preferred_element_type=jnp.float32
+        latf[:, i * rank : (i + 1) * rank] = lax.dot_general(
+            blocks[i],
+            basis[i // 2, i % 2],
+            (((1,), (1,)), ((), ())),
+            preferred_element_type=jnp.float32,
         )
     lat = latf[...]
     lat_ref[...] = lat.astype(lat_ref.dtype)
@@ -206,16 +221,6 @@
             finish()
 
     butterfly(0).start()
-    loads[4].wait()
-
-    def turn(h, carry):
-        at = pl.ds(pl.multiple_of(h * hd, hd), hd)
-        to = pl.ds(pl.multiple_of(h * rows, rows), rows)
-        qt[:, to] = qbuf[:, at].T
-        return carry
-
-    lax.fori_loop(0, heads * group, turn, 0)
-
     def attend(d):
         def work():
             seg_q = jnp.broadcast_to(segbuf[0].astype(jnp.float32), (rows, rows))
@@ -260,7 +265,7 @@
                     acc[:, at] = mixed
                     return carry
 
-                lax.fori_loop(0, chunks, one, 0)
+                lax.fori_loop(0, chunks, one, 0, unroll=unroll)
 
         if d == 0:
             work()
@@ -289,21 +294,33 @@
     if reach > last_even:
         attend(reach)
 
-    def settle(h, carry):
-        at = pl.ds(pl.multiple_of(h * rows, rows), rows)
-        to = pl.ds(pl.multiple_of(h * hd, hd), hd)
-        mixed = acc[:, at] * (1.0 / sums[:, at])
-        outv[:, to] = mixed.T.astype(outv.dtype)
-        return carry
-
-    lax.fori_loop(0, heads * group, settle, 0)
-    store = pltpu.make_async_copy(outv, att_hbm, out_sem)
-    store.start()
+    for g in range(heads):
+        at = slice(g * group * rows, (g + 1) * group * rows)
+        att_ref[:, at] = (acc[:, at] * (1.0 / sums[:, at])).astype(att_ref.dtype)
     for e in range(0, reach + 1, 2):
         for which in range(3):
             for ok, copy in copies(e, which):
                 pl.when(ok)(copy.wait_send)
-    store.wait()
+
+
+def place(
+    heads, group, hd, mixed_ref, lat_in, cap_in, share_in,
+    att_hbm, lat_ref, cap_ref, share_ref, outv, sem,
+):
+    rows = outv.shape[0]
+    stores = []
+    for g in range(heads):
+        for h in range(g * group, (g + 1) * group):
+            outv[:, h * hd : (h + 1) * hd] = mixed_ref[:, h * rows : (h + 1) * rows].T
+        cols = pl.ds(g * group * hd, group * hd)
+        store = pltpu.make_async_copy(outv.at[:, cols], att_hbm.at[:, cols], sem.at[g])
+        store.start()
+        stores.append(store)
+    lat_ref[...] = lat_in[...]
+    cap_ref[...] = cap_in[...]
+    share_ref[...] = share_in[...]
+    for store in stores:
+        store.wait()
 
 
 def body(n, kv_n, queries, keys, values, segments, basis):
@@ -316,37 +333,35 @@
     lanes = heads * group * rows
     f32, bf16 = jnp.float32, jnp.bfloat16
     dma = pltpu.SemaphoreType.DMA
-    any_space = pl.BlockSpec(memory_space=pl.ANY)
+    hbm = pl.BlockSpec(memory_space=pltpu.HBM)
     vmem = pl.BlockSpec(memory_space=pltpu.VMEM)
-    return pl.pallas_call(
+    mixed, lat, cap, share = pl.pallas_call(
         functools.partial(kernel, n, kv_n, reach, heads, group, hd, rank),
         out_shape=(
-            jax.ShapeDtypeStruct(queries.shape, bf16),
+            jax.ShapeDtypeStruct((hd, lanes), bf16),
             jax.ShapeDtypeStruct((rows, heads * 2 * rank), bf16),
             jax.ShapeDtypeStruct((heads, 2, rank, rank), f32),
             jax.ShapeDtypeStruct((heads, 2), f32),
         ),
-        in_specs=[any_space] * 5,
-        out_specs=(any_space, vmem, vmem, vmem),
+        in_specs=[hbm] * 5,
+        out_specs=(vmem, vmem, vmem, vmem),
         scratch_shapes=[
             pltpu.VMEM(queries.shape, bf16),
             pltpu.VMEM((hd, lanes), bf16),
             pltpu.VMEM((reach + 1, rows, width), bf16),
             pltpu.VMEM((reach + 1, rows, width), bf16),
             pltpu.VMEM((reach + 1, 1, rows), jnp.int32),
-            pltpu.VMEM(basis.shape, bf16),
+            pltpu.VMEM((heads, 2, rank, hd), bf16),
             pltpu.VMEM((heads, hd, rows), bf16),
             pltpu.VMEM((rows, 2 * rows), f32),
             pltpu.VMEM((1, lanes), f32),
             pltpu.VMEM((1, lanes), f32),
             pltpu.VMEM((hd, lanes), f32),
-            pltpu.VMEM(queries.shape, bf16),
             pltpu.VMEM((rows, 2 * heads * rank), f32),
             pltpu.VMEM((rounds + 1, rank + 8, hd), f32),
             pltpu.VMEM((rounds, rank + 8, hd), f32),
             pltpu.VMEM((kv_n, 8, hd), f32),
             dma((5,)),
-            dma,
             dma((reach + 1, 3, 3)),
             dma((reach + 1, 3)),
             dma((rounds,)),
@@ -354,8 +369,23 @@
             dma((kv_n,)),
             dma((kv_n,)),
         ],
-        compiler_params=pltpu.CompilerParams(collective_id=0, has_side_effects=True),
-    )(queries, keys, values, segments.reshape(1, rows), basis)
+        compiler_params=pltpu.CompilerParams(
+            collective_id=0, has_side_effects=True, vmem_limit_bytes=LIMIT
+        ),
+    )(queries, keys, values, segments.reshape(1, rows), jnp.swapaxes(basis, 2, 3))
+    return pl.pallas_call(
+        functools.partial(place, heads, group, hd),
+        out_shape=(
+            jax.ShapeDtypeStruct(queries.shape, bf16),
+            jax.ShapeDtypeStruct(lat.shape, lat.dtype),
+            jax.ShapeDtypeStruct(cap.shape, cap.dtype),
+            jax.ShapeDtypeStruct(share.shape, share.dtype),
+        ),
+        in_specs=[vmem] * 4,
+        out_specs=(hbm, vmem, vmem, vmem),
+        scratch_shapes=[pltpu.VMEM(queries.shape, bf16), dma((heads,))],
+        compiler_params=pltpu.CompilerParams(vmem_limit_bytes=LIMIT),
+    )(mixed, lat, cap, share)
 
 
 def solution(mesh):

time: 35.4 us -> 28.1 us (0.79)
  the two profiles are of different devices: /device:TPU:20 before, /device:TPU:13 now
where the time goes in v2:
time: 28.1 us; the launch traced here: 27.8 us
  Pallas kernels  23 us (82%)
  local copies, waits for them, and re-layouts  4.12 us (15%)
  between operations  0.65 us (2%)
    pallas_call x1, Pallas kernels, body(): pl.pallas_call(functools.partial(kernel, n, kv_n, reach, heads, group, hd...  21.4 us
    unnamed x10, local copies, waits for them, and re-layouts  4.12 us
    pallas_call x1, Pallas kernels, body(): pl.pallas_call(functools.partial(place, heads, group, hd), out_shape=(jax...  1.57 us

profile of v2, /device:TPU:13, one launch (start us, length us, event | category | flops | bytes accessed | tf_op | source)
XLA Modules:
  0.0 27.8 jit_solution(5209134707873323768)
XLA Ops:
  0.6 0.0 copy-start.4
  0.6 0.6 %copy-done.4 = s32[128]{0:T(128)S(1)} copy-done((s32[128]{0:T(128)S(1)}, s32[128]{0:T(128)}, u32[]{:S(2)}) %copy-start.4) | copy-done | bytes 536
  1.3 0.0 copy-start
  1.3 1.0 %copy-done = bf16[128,2048]{1,0:T(8,128)(2,1)S(1)} copy-done((bf16[128,2048]{1,0:T(8,128)(2,1)S(1)}, bf16[128,2048]{1,0:T(8,128)(2,1)}, u32[]{:S(2)}) %copy-start) | copy-done | bytes 524312
  2.3 0.0 copy-start.1
  2.3 0.8 %copy-done.1 = bf16[128,256]{1,0:T(8,128)(2,1)S(1)} copy-done((bf16[128,256]{1,0:T(8,128)(2,1)S(1)}, bf16[128,256]{1,0:T(8,128)(2,1)}, u32[]{:S(2)}) %copy-start.1) | copy-done | bytes 65560
  3.2 0.0 copy-start.2
  3.2 0.8 %copy-done.2 = bf16[128,256]{1,0:T(8,128)(2,1)S(1)} copy-done((bf16[128,256]{1,0:T(8,128)(2,1)S(1)}, bf16[128,256]{1,0:T(8,128)(2,1)}, u32[]{:S(2)}) %copy-start.2) | copy-done | bytes 65560
  4.0 0.0 copy-start.3
  4.0 0.8 %copy-done.3 = bf16[2,2,128,32]{2,3,1,0:T(8,128)(2,1)S(1)} copy-done((bf16[2,2,128,32]{2,3,1,0:T(8,128)(2,1)S(1)}, bf16[2,2,128,32]{2,3,1,0:T(8,128)(2,1)}, u32[]{:S(2)}) %copy-start.3) | copy-done | bytes 32792
  4.8 21.4 %shard_map.84 = (bf16[128,2048]{1,0:T(8,128)(2,1)S(1)}, bf16[128,128]{1,0:T(8,128)(2,1)S(1)}, f32[2,2,32,32]{3,2,1,0:T(8,128)S(1)}, f32[2,2]{1,0:T(2,128)S(1)}) custom-call(bf16[128,2048]{1,0:T(8,128)(2,1)S(1)} %copy-done, bf16[128,256]{1,0:T(8,128)(2,1)S(1)} %copy-done.1, bf16[128,256]{1,0:T(8,128)(2,1)S(1)} %copy-done.2, s32[1,128]{1,0:T(1,128)S(1)} %bitcast.3, ...), custom_call_target="tpu_custom_call" | custom-call | tf_op jit(solution)/shard_map/pallas_call | solution.py:338
  26.2 1.6 %shard_map.85 = (bf16[128,2048]{1,0:T(8,128)(2,1)}, bf16[128,128]{1,0:T(8,128)(2,1)}, f32[2,2,32,32]{3,2,1,0:T(8,128)}, f32[2,2]{1,0:T(2,128)}) custom-call(bf16[128,2048]{1,0:T(8,128)(2,1)S(1)} %get-tuple-element.8.mixed_ref, bf16[128,128]{1,0:T(8,128)(2,1)S(1)} %get-tuple-element.9.lat_in, f32[2,2,32,32]{3,2,1,0:T(8,128)S(1)} %get-tuple-element.10.cap_in, ...), custom_call_target="tpu_custom_call" | custom-call | tf_op jit(solution)/shard_map/pallas_call | solution.py:376
Async XLA Ops:
  0.6 0.7 %copy-start.4 = (s32[128]{0:T(128)S(1)}, s32[128]{0:T(128)}, u32[]{:S(2)}) copy-start(s32[128]{0:T(128)} %param.8) | copy-start | bytes 1540
  1.3 1.0 %copy-start = (bf16[128,2048]{1,0:T(8,128)(2,1)S(1)}, bf16[128,2048]{1,0:T(8,128)(2,1)}, u32[]{:S(2)}) copy-start(bf16[128,2048]{1,0:T(8,128)(2,1)} %q_hbm.1) | copy-start | bytes 1572868
  2.3 0.8 %copy-start.1 = (bf16[128,256]{1,0:T(8,128)(2,1)S(1)}, bf16[128,256]{1,0:T(8,128)(2,1)}, u32[]{:S(2)}) copy-start(bf16[128,256]{1,0:T(8,128)(2,1)} %k_hbm.1) | copy-start | bytes 196612
  3.2 0.8 %copy-start.2 = (bf16[128,256]{1,0:T(8,128)(2,1)S(1)}, bf16[128,256]{1,0:T(8,128)(2,1)}, u32[]{:S(2)}) copy-start(bf16[128,256]{1,0:T(8,128)(2,1)} %v_hbm.1) | copy-start | bytes 196612
  4.0 0.8 %copy-start.3 = (bf16[2,2,128,32]{2,3,1,0:T(8,128)(2,1)S(1)}, bf16[2,2,128,32]{2,3,1,0:T(8,128)(2,1)}, u32[]{:S(2)}) copy-start(bf16[2,2,128,32]{2,3,1,0:T(8,128)(2,1)} %param.9) | copy-start | bytes 98308

commit v3 on v2

--- a/solution.py
+++ b/solution.py
@@ -29,7 +29,7 @@
     me = lax.axis_index("seq")
     kv = lax.axis_index("kvh")
     odd = lax.rem(me, 2)
-    rows = kbuf.shape[1]
+    rows = kbuf.shape[2]
     rounds = int(math.log2(n))
     scale = float(hd) ** -0.5 * math.log2(math.e)
     wide = 2 * rows
@@ -41,11 +41,14 @@
         pltpu.make_async_copy(src, dst, in_sem.at[i])
         for i, (src, dst) in enumerate(
             [
-                (k_hbm, kbuf.at[0]),
-                (v_hbm, vbuf.at[0]),
                 (seg_hbm, segbuf.at[0]),
                 (basis_hbm, basis),
                 (q_hbm, qbuf),
+            ]
+            + [
+                (src.at[:, pl.ds(g * hd, hd)], dst.at[0, g])
+                for g in range(heads)
+                for src, dst in ((k_hbm, kbuf), (v_hbm, vbuf))
             ]
         )
     ]
@@ -75,7 +78,9 @@
         pl.semaphore_signal(
             barrier, inc=1, device_id={"kvh": lax.rem(kv + o, kv_n)}, device_id_type=MESH
         )
-    loads[4].wait()
+
+    for load in loads:
+        load.wait()
 
     def turn(h, carry):
         at = pl.ds(pl.multiple_of(h * hd, hd), hd)
@@ -85,66 +90,9 @@
 
     lax.fori_loop(0, heads * group, turn, 0, unroll=unroll)
 
-    pl.semaphore_wait(barrier, count + (rounds - 2) + (kv_n - 1))
-
-    bufs = (segbuf, kbuf, vbuf)
-    own = (seg_hbm, k_hbm, v_hbm)
-
-    def routes(e):
-        out = []
-        if e + 2 <= reach:
-            out.append((0, 2, me + 2 < n))
-        if e + 1 <= reach:
-            out.append((1, 1, odd == 0))
-        if e >= 2:
-            out.append((1, -1, odd == 1))
-        if e + 1 == reach:
-            out.append((2, 1, (odd == 1) & (me + 1 < n)))
-        return out
-
-    def copies(e, which):
-        found = []
-        for lane, step, ok in routes(e):
-            src = own[which] if e == 0 else bufs[which].at[e]
-            copy = remote(
-                src,
-                bufs[which].at[e + step],
-                send_sem.at[e, lane, which],
-                recv_sem.at[e + step, which],
-                {"seq": me + step},
-            )
-            found.append((ok & (me >= e), copy))
-        return found
-
-    def send(e, which):
-        for ok, copy in copies(e, which):
-            pl.when(ok)(copy.start)
-
-    def receive(d, which):
-        copy = remote(
-            bufs[which].at[0],
-            bufs[which].at[d],
-            send_sem.at[0, 0, which],
-            recv_sem.at[d, which],
-            {"seq": me},
-        )
-        pl.when(me >= d)(copy.wait_recv)
-
-    def forward(e):
-        for which in range(3):
-            receive(e, which)
-            send(e, which)
-
-    for which in (1, 2, 0):
-        send(0, which)
-
-    for load in loads[:4]:
-        load.wait()
-
     blocks = []
     for g in range(heads):
-        cols = slice(g * hd, (g + 1) * hd)
-        blocks += [kbuf[0, :, cols], vbuf[0, :, cols]]
+        blocks += [kbuf[0, g], vbuf[0, g]]
     for i in range(parts):
         latf[:, i * rank : (i + 1) * rank] = lax.dot_general(
             blocks[i],
@@ -173,6 +121,59 @@
         squares = jnp.where(row == i, jnp.sum(block * block, axis=0, keepdims=True), squares)
     mine[0, rank:, :] = squares
 
+    pl.semaphore_wait(barrier, count + (rounds - 2) + (kv_n - 1))
+
+    pieces = 1 + parts
+
+    def piece(d, which):
+        if which == 0:
+            return segbuf.at[d]
+        return (kbuf, vbuf)[(which - 1) % 2].at[d, (which - 1) // 2]
+
+    def routes(e):
+        out = []
+        if e + 2 <= reach:
+            out.append((0, 2, me + 2 < n))
+        if e + 1 <= reach:
+            out.append((1, 1, odd == 0))
+        if e >= 2:
+            out.append((1, -1, odd == 1))
+        if e + 1 == reach:
+            out.append((2, 1, (odd == 1) & (me + 1 < n)))
+        return out
+
+    def copies(e, which):
+        found = []
+        for lane, step, ok in routes(e):
+            copy = remote(
+                piece(e, which),
+                piece(e + step, which),
+                send_sem.at[e, lane, which],
+                recv_sem.at[e + step, which],
+                {"seq": me + step},
+            )
+            found.append((ok & (me >= e), copy))
+        return found
+
+    def send(e, which):
+        for ok, copy in copies(e, which):
+            pl.when(ok)(copy.start)
+
+    def receive(d, which):
+        copy = remote(
+            piece(0, which),
+            piece(d, which),
+            send_sem.at[0, 0, which],
+            recv_sem.at[d, which],
+            {"seq": me},
+        )
+        pl.when(me >= d)(copy.wait_recv)
+
+    def forward(e):
+        for which in range(pieces):
+            receive(e, which)
+            send(e, which)
+
     def butterfly(r):
         return remote(mine.at[r], theirs.at[r], bf_send.at[r], bf_recv.at[r], {"seq": partner(r)})
 
@@ -221,6 +222,8 @@
             finish()
 
     butterfly(0).start()
+    for which in range(pieces):
+        send(0, which)
     def attend(d):
         def work():
             seg_q = jnp.broadcast_to(segbuf[0].astype(jnp.float32), (rows, rows))
@@ -235,14 +238,15 @@
             bias[:, :rows] = hidden
             bias[:, rows:] = hidden
             for g in range(heads):
-                vt[g] = vbuf[d, :, g * hd : (g + 1) * hd].T
-
-            for g in range(heads):
+                if d % 2 == 1:
+                    receive(d, 2 * g + 1)
+                    receive(d, 2 * g + 2)
+                vt[g] = vbuf[d, g].T
 
                 def one(c, carry, g=g):
                     at = pl.ds(pl.multiple_of(g * group * rows + c * wide, wide), wide)
                     scores = jnp.dot(
-                        kbuf[d, :, g * hd : (g + 1) * hd],
+                        kbuf[d, g],
                         qt[:, at],
                         preferred_element_type=jnp.float32,
                     )
@@ -274,18 +278,17 @@
             @pl.when(me >= d)
             def _():
                 if d % 2 == 1:
-                    for which in range(3):
-                        receive(d, which)
+                    receive(d, 0)
                 work()
 
     attend(0)
+    advance()
     for e in range(2, reach + 1, 2):
         forward(e)
         advance()
         if e >= 4:
             attend(e - 3)
         attend(e)
-        advance()
     last_even = reach - reach % 2
     if last_even >= 2:
         attend(last_even - 1)
@@ -298,7 +301,7 @@
         at = slice(g * group * rows, (g + 1) * group * rows)
         att_ref[:, at] = (acc[:, at] * (1.0 / sums[:, at])).astype(att_ref.dtype)
     for e in range(0, reach + 1, 2):
-        for which in range(3):
+        for which in range(pieces):
             for ok, copy in copies(e, which):
                 pl.when(ok)(copy.wait_send)
 
@@ -329,7 +332,6 @@
     group = queries.shape[1] // (heads * hd)
     reach = min(n - 1, n // 2 + 1)
     rounds = int(math.log2(n))
-    width = heads * hd
     lanes = heads * group * rows
     f32, bf16 = jnp.float32, jnp.bfloat16
     dma = pltpu.SemaphoreType.DMA
@@ -348,8 +350,8 @@
         scratch_shapes=[
             pltpu.VMEM(queries.shape, bf16),
             pltpu.VMEM((hd, lanes), bf16),
-            pltpu.VMEM((reach + 1, rows, width), bf16),
-            pltpu.VMEM((reach + 1, rows, width), bf16),
+            pltpu.VMEM((reach + 1, heads, rows, hd), bf16),
+            pltpu.VMEM((reach + 1, heads, rows, hd), bf16),
             pltpu.VMEM((reach + 1, 1, rows), jnp.int32),
             pltpu.VMEM((heads, 2, rank, hd), bf16),
             pltpu.VMEM((heads, hd, rows), bf16),
@@ -361,9 +363,9 @@
             pltpu.VMEM((rounds + 1, rank + 8, hd), f32),
             pltpu.VMEM((rounds, rank + 8, hd), f32),
             pltpu.VMEM((kv_n, 8, hd), f32),
-            dma((5,)),
-            dma((reach + 1, 3, 3)),
-            dma((reach + 1, 3)),
+            dma((3 + 2 * heads,)),
+            dma((reach + 1, 3, 1 + 2 * heads)),
+            dma((reach + 1, 1 + 2 * heads)),
             dma((rounds,)),
             dma((rounds,)),
             dma((kv_n,)),
@@ -372,7 +374,10 @@
         compiler_params=pltpu.CompilerParams(
             collective_id=0, has_side_effects=True, vmem_limit_bytes=LIMIT
         ),
-    )(queries, keys, values, segments.reshape(1, rows), jnp.swapaxes(basis, 2, 3))
+    )(*[
+        pltpu.with_memory_space_constraint(x, pltpu.HBM)
+        for x in (queries, keys, values, segments.reshape(1, rows), jnp.swapaxes(basis, 2, 3))
+    ])
     return pl.pallas_call(
         functools.partial(place, heads, group, hd),
         out_shape=(

time: 28.1 us -> 21.3 us (0.76)
  the two profiles are of different devices: /device:TPU:13 before, /device:TPU:0 now
where the time goes in v3:
time: 21.3 us; the launch traced here: 21.2 us
  Pallas kernels  20.6 us (97%)
  between operations  0.64 us (3%)
    pallas_call x1, Pallas kernels, body(): pl.pallas_call(functools.partial(kernel, n, kv_n, reach, heads, group, hd...  19 us
    pallas_call x1, Pallas kernels, body(): pl.pallas_call(functools.partial(place, heads, group, hd), out_shape=(jax...  1.57 us

profile of v3, /device:TPU:0, one launch (start us, length us, event | category | flops | bytes accessed | tf_op | source)
XLA Modules:
  0.0 21.2 jit_solution(8523173642832999253)
XLA Ops:
  0.6 19.0 %shard_map.84 = (bf16[128,2048]{1,0:T(8,128)(2,1)S(1)}, bf16[128,128]{1,0:T(8,128)(2,1)S(1)}, f32[2,2,32,32]{3,2,1,0:T(8,128)S(1)}, f32[2,2]{1,0:T(2,128)S(1)}) custom-call(bf16[128,2048]{1,0:T(8,128)(2,1)} %q_hbm.1, bf16[128,256]{1,0:T(8,128)(2,1)} %k_hbm.1, bf16[128,256]{1,0:T(8,128)(2,1)} %v_hbm.1, s32[1,128]{1,0:T(1,128)} %bitcast.3, ...), custom_call_target="tpu_custom_call" | custom-call | tf_op jit(solution)/shard_map/pallas_call | solution.py:340
  19.6 1.6 %shard_map.85 = (bf16[128,2048]{1,0:T(8,128)(2,1)}, bf16[128,128]{1,0:T(8,128)(2,1)}, f32[2,2,32,32]{3,2,1,0:T(8,128)}, f32[2,2]{1,0:T(2,128)}) custom-call(bf16[128,2048]{1,0:T(8,128)(2,1)S(1)} %get-tuple-element.8.mixed_ref, bf16[128,128]{1,0:T(8,128)(2,1)S(1)} %get-tuple-element.9.lat_in, f32[2,2,32,32]{3,2,1,0:T(8,128)S(1)} %get-tuple-element.10.cap_in, ...), custom_call_target="tpu_custom_call" | custom-call | tf_op jit(solution)/shard_map/pallas_call | solution.py:381

commit v4 on v3

--- a/solution.py
+++ b/solution.py
@@ -175,51 +175,63 @@
             send(e, which)
 
     def butterfly(r):
-        return remote(mine.at[r], theirs.at[r], bf_send.at[r], bf_recv.at[r], {"seq": partner(r)})
+        return remote(
+            mine.at[r + min(r, 1)], theirs.at[r], bf_send.at[r], bf_recv.at[r], {"seq": partner(r)})
 
     def spread(o):
         return remote(
-            mine.at[rounds, pl.ds(rank, 8)],
+            mine.at[1, pl.ds(rank, 8)],
             ebuf.at[o],
             e_send.at[o],
             e_recv.at[o],
             {"kvh": lax.rem(kv + o, kv_n)},
         )
 
-    def finish():
+    def gather():
         for o in range(1, kv_n):
             spread(o).wait()
-        energy = mine[rounds, rank:, :]
+        energy = mine[1, rank:, :]
         total = energy
         for o in range(1, kv_n):
             total = total + ebuf[o]
-        energy = jnp.sum(energy, axis=1, keepdims=True)
-        total = jnp.sum(total, axis=1, keepdims=True)
         for c in range(2):
             whole = total[c : c + 1]
             for g in range(1, heads):
                 whole = whole + total[2 * g + c : 2 * g + c + 1]
-            for g in range(heads):
-                i = 2 * g + c
-                share_ref[g : g + 1, c : c + 1] = (heads * kv_n) * energy[i : i + 1] / whole
+            energy = jnp.where(row == parts + c, whole, energy)
+        mine[2, :rank, :] = mine[1, :rank, :]
+        mine[2, rank:, :] = energy
+
+    def finish():
+        final = rounds + 1
+        energy = jnp.sum(mine[final, rank:, :], axis=1, keepdims=True)
         for i in range(parts):
-            cap_ref[i // 2, i % 2] = mine[rounds, :rank, i * rank : (i + 1) * rank] / (rows * n)
+            c = parts + i % 2
+            share_ref[i // 2 : i // 2 + 1, i % 2 : i % 2 + 1] = (
+                (heads * kv_n) * energy[i : i + 1] / energy[c : c + 1]
+            )
+            cap_ref[i // 2, i % 2] = mine[final, :rank, i * rank : (i + 1) * rank] / (rows * n)
 
     stage = [0]
 
     def advance():
         r = stage[0]
         stage[0] += 1
-        if r < rounds:
-            butterfly(r).wait()
-            mine[r + 1] = mine[r] + theirs[r]
-            if r + 1 < rounds:
-                butterfly(r + 1).start()
+        if r == 0:
+            butterfly(0).wait()
+            mine[1] = mine[0] + theirs[0]
+            for o in range(1, kv_n):
+                spread(o).start()
+        elif r == 1:
+            gather()
+            butterfly(1).start()
+        elif r <= rounds:
+            butterfly(r - 1).wait()
+            mine[r + 1] = mine[r] + theirs[r - 1]
+            if r < rounds:
+                butterfly(r).start()
             else:
-                for o in range(1, kv_n):
-                    spread(o).start()
-        elif r == rounds:
-            finish()
+                finish()
 
     butterfly(0).start()
     for which in range(pieces):
@@ -360,7 +372,7 @@
             pltpu.VMEM((1, lanes), f32),
             pltpu.VMEM((hd, lanes), f32),
             pltpu.VMEM((rows, 2 * heads * rank), f32),
-            pltpu.VMEM((rounds + 1, rank + 8, hd), f32),
+            pltpu.VMEM((rounds + 2, rank + 8, hd), f32),
             pltpu.VMEM((rounds, rank + 8, hd), f32),
             pltpu.VMEM((kv_n, 8, hd), f32),
             dma((3 + 2 * heads,)),

time: 21.3 us -> 21.3 us (level)
  no operation moved by 1% of the time
where the time goes in v4:
time: 21.3 us; the launch traced here: 21 us
  Pallas kernels  20.4 us (96%)
  between operations  0.64 us (3%)
    pallas_call x1, Pallas kernels, body(): pl.pallas_call(functools.partial(kernel, n, kv_n, reach, heads, group, hd...  18.8 us
    pallas_call x1, Pallas kernels, body(): pl.pallas_call(functools.partial(place, heads, group, hd), out_shape=(jax...  1.57 us

profile of v4, /device:TPU:0, one launch (start us, length us, event | category | flops | bytes accessed | tf_op | source)
XLA Modules:
  0.0 21.0 jit_solution(1034380505082386879)
XLA Ops:
  0.6 18.8 %shard_map.84 = (bf16[128,2048]{1,0:T(8,128)(2,1)S(1)}, bf16[128,128]{1,0:T(8,128)(2,1)S(1)}, f32[2,2,32,32]{3,2,1,0:T(8,128)S(1)}, f32[2,2]{1,0:T(2,128)S(1)}) custom-call(bf16[128,2048]{1,0:T(8,128)(2,1)} %q_hbm.1, bf16[128,256]{1,0:T(8,128)(2,1)} %k_hbm.1, bf16[128,256]{1,0:T(8,128)(2,1)} %v_hbm.1, s32[1,128]{1,0:T(1,128)} %bitcast.3, ...), custom_call_target="tpu_custom_call" | custom-call | tf_op jit(solution)/shard_map/pallas_call | solution.py:352
  19.4 1.6 %shard_map.85 = (bf16[128,2048]{1,0:T(8,128)(2,1)}, bf16[128,128]{1,0:T(8,128)(2,1)}, f32[2,2,32,32]{3,2,1,0:T(8,128)}, f32[2,2]{1,0:T(2,128)}) custom-call(bf16[128,2048]{1,0:T(8,128)(2,1)S(1)} %get-tuple-element.8.mixed_ref, bf16[128,128]{1,0:T(8,128)(2,1)S(1)} %get-tuple-element.9.lat_in, f32[2,2,32,32]{3,2,1,0:T(8,128)S(1)} %get-tuple-element.10.cap_in, ...), custom_call_target="tpu_custom_call" | custom-call | tf_op jit(solution)/shard_map/pallas_call | solution.py:393
